TPU v7x, 32 devices: a whole 2x2x4 slice. The times are simulated.
32 devices in a mesh: groups: 2 (over x), seq: 16 (over z, y, core).
Axes of the slice: x: 2, y: 2, z: 4, core: 2. Of those that a mesh axis runs over, the one named last changes fastest.
Arguments:
- query_block: bfloat16 [512, 4096], P(('groups', 'seq')), parts along dimension 0, may hold values from -112 to 112
- cache_keys: bfloat16 [8192, 2048], P(('groups', 'seq')), parts along dimension 0, may hold values from -4 to 4
- stored_values: bfloat16 [8192, 2048], P(('groups', 'seq')), parts along dimension 0, may hold values from -6 to 6
- live_counts: int32 [32], P(('groups', 'seq')), parts along dimension 0, may hold values from 128 to 256
- first_position: int32 [2], P('groups'), parts along dimension 0, may hold values from 0 to 3840
- out_weight: bfloat16 [4096, 5376], P('seq'), may hold values from -0.09375 to 0.09375
Outputs:
- attended: bfloat16 [512, 5376], P(('groups', 'seq')), parts along dimension 0
There are 2 independent parts, one for each index of `groups`. A program takes and returns all parts, laid end to end along the dimension named above; an argument that names none is the same for every part. Nothing has to cross between parts.
Inputs may be any that keep to these rules, and one draw needn't show every extreme that they name: `live_counts`: the live slots of a block are its first ones.
All inputs are finite; a program needn't handle non-finite values.
Results may differ from a plain program's by a relative error of at most 0.0058.
Values may be sent and summed in bfloat16 or wider, within the bound.
A program may use at most 64 MiB of HBM per device.

v0:
```python
import jax
import jax.numpy as jnp
from jax import lax
from jax.sharding import PartitionSpec as P

QUERY_HEADS = 32
KEY_VALUE_HEADS = 16
HEAD_SIZE = 128


score_scale = 168.0 ** (-0.5)
masked_value = -1e30


def head_partial(query_cols, key_cols, value_cols, allowed, group_width):
    row_count = query_cols.shape[0]
    grouped = query_cols.reshape(row_count, group_width, HEAD_SIZE)
    scores = (
        jnp.einsum("rgd,kd->grk", grouped, key_cols, preferred_element_type=jnp.float32)
        * score_scale
    )
    row_best = jnp.max(jnp.where(allowed[None], scores, masked_value), axis=2)
    shifted = jnp.where(allowed[None], scores - row_best[:, :, None], -jnp.inf)
    weights = jnp.exp(shifted)
    weight_sum = jnp.sum(weights, axis=2)
    safe_total = jnp.where(weight_sum > 0, weight_sum, 1.0)
    weighted = jnp.einsum(
        "grk,kd->grd", weights.astype(jnp.bfloat16), value_cols, preferred_element_type=jnp.float32
    )
    value_partial_sum = (weighted / safe_total[:, :, None]).astype(jnp.bfloat16)
    log_sum_exp = jnp.where(weight_sum > 0, row_best + jnp.log(safe_total), masked_value)
    return (value_partial_sum, log_sum_exp)


def merge_sources(received, totals):
    largest = jnp.max(totals, axis=0)
    scales = jnp.exp(totals - largest[None])
    blended = jnp.sum(scales[..., None] * received.astype(jnp.float32), axis=0)
    return (blended / jnp.sum(scales, axis=0)[..., None]).astype(jnp.bfloat16)


def body(query_block, cache_keys, stored_values, live_counts, first_position, out_weight):
    devices = lax.axis_size("seq")
    source = lax.axis_index("seq")
    key_count = cache_keys.shape[0]
    row_total = query_block.shape[0] * devices
    per_group = QUERY_HEADS // devices
    group_width = QUERY_HEADS // KEY_VALUE_HEADS
    first_key = source * key_count
    live_count = live_counts[0]
    begin_pos = first_position[0]
    key_index = lax.iota(jnp.int32, key_count)
    piece_rows = lax.all_gather(query_block, "seq", axis=0, tiled=True)
    row_count = piece_rows.shape[0]
    query_pos = begin_pos + lax.iota(jnp.int32, row_count)
    allowed = (key_index[None, :] < live_count) & (
        first_key + key_index[None, :] <= query_pos[:, None]
    )

    def single_head(key_value_head):
        query_cols = lax.dynamic_slice_in_dim(
            piece_rows, key_value_head * (group_width * HEAD_SIZE), group_width * HEAD_SIZE, 1
        )
        key_cols = lax.dynamic_slice_in_dim(cache_keys, key_value_head * HEAD_SIZE, HEAD_SIZE, 1)
        value_cols = lax.dynamic_slice_in_dim(
            stored_values, key_value_head * HEAD_SIZE, HEAD_SIZE, 1
        )
        return head_partial(query_cols, key_cols, value_cols, allowed, group_width)

    value_partial_sum, log_sum_exp = lax.map(
        single_head, jnp.arange(KEY_VALUE_HEADS, dtype=jnp.int32)
    )
    value_partial_sum = jnp.transpose(value_partial_sum, (2, 0, 1, 3)).reshape(
        row_count, QUERY_HEADS, HEAD_SIZE
    )
    log_sum_exp = jnp.transpose(log_sum_exp, (2, 0, 1)).reshape(row_count, QUERY_HEADS)
    value_partial_sum, log_sum_exp = (value_partial_sum, log_sum_exp)
    value_partial_sum, log_sum_exp = (value_partial_sum, log_sum_exp)
    received = lax.all_to_all(
        value_partial_sum[None], "seq", split_axis=2, concat_axis=0, tiled=True
    )
    totals = lax.all_to_all(log_sum_exp[None], "seq", split_axis=2, concat_axis=0, tiled=True)
    merged = merge_sources(received, totals)
    flattened = merged.reshape(row_total, per_group * HEAD_SIZE)
    summed = lax.psum_scatter(
        jnp.dot(flattened, out_weight, preferred_element_type=jnp.float32),
        "seq",
        scatter_dimension=0,
        tiled=True,
    )
    return summed.astype(jnp.bfloat16)


def solution(mesh):
    in_specs = (
        P(("groups", "seq"), None),
        P(("groups", "seq"), None),
        P(("groups", "seq"), None),
        P(("groups", "seq")),
        P("groups"),
        P("seq", None),
    )
    out_specs = P(("groups", "seq"), None)
    return jax.shard_map(body, mesh=mesh, in_specs=in_specs, out_specs=out_specs, check_vma=False)
```

profile of v0, /device:TPU:0, one launch (start us, length us, event | category | flops | bytes accessed | tf_op | source)
XLA Modules:
  0.0 307.4 jit_solution(6038253713847439832)
XLA Ops:
  8.7 45.0 %all-gather.2.cloned.1.call-done = bf16[256,4096]{1,0:T(8,128)(2,1)} async-done(((bf16[16,4096]{1,0:T(8,128)(2,1)}), bf16[256,4096]{1,0:T(8,128)(2,1)}) %all-gather.2.cloned.1.call-update) | async-done | bytes 2097168 | tf_op jit(solution)/shard_map/all_gather | solution.py:53
  53.7 97.2 %while.13 = (s32[]{:T(128)}, bf16[16,2,256,128]{3,2,1,0:T(8,128)(2,1)}, f32[16,2,256]{2,1,0:T(2,128)S(1)}, s32[16]{0:T(128)S(1)}, bf16[256,2048]{1,0:T(8,128)(2,...) while((s32[]{:T(128)}, ...), condition=%wide.region_3.4_spmd.clone, body=%wide.region_0.3_spmd.clone.sunk | while | flops 68552712 | bytes 2775577 | solution.py:70
  58.0 1.8 fusion.40
  64.0 1.8 fusion.40
  70.1 1.8 fusion.40
  76.2 1.8 fusion.40
  82.3 1.8 fusion.40
  88.3 1.8 fusion.40
  94.4 1.8 fusion.40
  100.5 1.8 fusion.40
  106.6 1.8 fusion.40
  112.6 1.8 fusion.40
  118.7 1.8 fusion.40
  124.8 1.8 fusion.40
  130.9 1.8 fusion.40
  136.9 1.8 fusion.40
  143.0 1.8 fusion.40
  149.1 1.8 fusion.40
  151.0 9.9 %all_to_all.27 = f32[1,256,32]{1,0,2:T(1,128)S(1)} all-to-all(f32[1,256,32]{1,0,2:T(1,128)S(1)} %broadcast_in_dim_reshape.6), channel_id=1, replica_groups=mesh['groups'=2,'seq'=16] {'seq'}, dimensions={2} | all-to-all | bytes 65536 | tf_op jit(solution)/shard_map/all_to_all | solution.py:82
  160.8 4.4 %all-to-all-start.1 = ((bf16[1,256,32,128]{3,1,0,2:T(8,128)(2,1)}), bf16[1,256,32,128]{3,1,0,2:T(8,128)(2,1)}, u32[]{:S(2)}, u32[]{:S(2)}) async-start(bf16[1,256,32,128]{3,1,0,2:T(8,128)(2,1)} %bitcast.71), calls=%async_computation.1 | async-start | bytes 4194304 | tf_op jit(solution)/shard_map/all_to_all | solution.py:79
  165.4 40.8 %all-to-all-done.1 = bf16[1,256,32,128]{3,1,0,2:T(8,128)(2,1)} async-done(((bf16[1,256,32,128]{3,1,0,2:T(8,128)(2,1)}), bf16[1,256,32,128]{3,1,0,2:T(8,128)(2,1)}, u32[]{:S(2)}, u32[]{:S(2)}) %all-to-all-start.1) | async-done | bytes 2097184 | tf_op jit(solution)/shard_map/all_to_all | solution.py:79
  206.2 2.5 fusion.22
  209.0 3.3 %fusion.26 = f32[256,5376]{1,0:T(8,128)} fusion(bf16[256,256]{0,1:T(8,128)(2,1)S(1)} %bitcast.72, bf16[256,5376]{1,0:T(8,128)(2,1)S(1)} %copy-done), kind=kOutput, calls=%fused_computation.39 | convolution fusion | flops 704643072 | bytes 8388608 | tf_op jit(solution)/shard_map/dot_general | solution.py:86
  212.4 86.6 %reduce-scatter.2.cloned.1.call-done = f32[16,5376]{1,0:T(8,128)} async-done(((f32[256,5376]{1,0:T(8,128)}), f32[16,5376]{1,0:T(8,128)}) %reduce-scatter.2.cloned.1.call-update) | async-done | bytes 344080 | tf_op jit(solution)/shard_map/reduce_scatter | solution.py:85
  (145 shorter events, 50.3 us)
Async XLA Ops:
  6.5 202.5 %copy-start = (bf16[256,5376]{1,0:T(8,128)(2,1)S(1)}, bf16[256,5376]{1,0:T(8,128)(2,1)}, u32[]{:S(2)}) copy-start(bf16[256,5376]{1,0:T(8,128)(2,1)} %param.13) | copy-start | bytes 8257540
  6.5 47.2 %all-gather.2.cloned.1.call-start = ((), (), s32[]{:S(2)}) async-start(), calls=%async_computation.3 | async-start | bytes 2228224 | tf_op jit(solution)/shard_map/all_gather | solution.py:53
  160.8 45.4 %all-to-all-start.1 = ((bf16[1,256,32,128]{3,1,0,2:T(8,128)(2,1)}), bf16[1,256,32,128]{3,1,0,2:T(8,128)(2,1)}, u32[]{:S(2)}, u32[]{:S(2)}) async-start(bf16[1,256,32,128]{3,1,0,2:T(8,128)(2,1)} %bitcast.71), calls=%async_computation.1 | async-start | bytes 4194304 | tf_op jit(solution)/shard_map/all_to_all | solution.py:79
  165.3 133.6 %reduce-scatter.2.cloned.1.call-start = ((), (), s32[]{:S(2)}) async-start(), calls=%async_computation.4 | async-start | bytes 5849088 | tf_op jit(solution)/shard_map/reduce_scatter | solution.py:85
Sparse Core Ops, SparseCore 0:
  9.5 44.1 all-gather.1
  212.5 86.3 reduce-scatter.1
where the time goes:
time: 310 us; the launch traced here: 307 us
  waiting for transfers between devices  173 us (56%)
  matrix products  49.7 us (16%)
  local copies, waits for them, and re-layouts  25.9 us (8%)
  loops' own time  20.5 us (7%)
  between operations  14.9 us (5%)
  blocking collectives  9.87 us (3%)
  other arithmetic  9 us (3%)
  starting transfers between devices  4.47 us (1%)
    reduce_scatter x1, waiting for transfers between devices, body(): lax.psum_scatter(jnp.dot(flattened, out_weight, preferred_element_type=jn...  86.6 us
    all_gather x1, waiting for transfers between devices, body(): piece_rows = lax.all_gather(query_block, 'seq', axis=0, tiled=True)  45 us
    all_to_all x1, waiting for transfers between devices, body(): lax.all_to_all(value_partial_sum[None], 'seq', split_axis=2, concat_axis=...  40.8 us
    dot_general x16, matrix products, head_partial(): jnp.einsum('grk,kd->grd', weights.astype(jnp.bfloat16), value_cols, prefe...  29.2 us
    another operation x1, loops' own time, body(): lax.map(single_head, jnp.arange(KEY_VALUE_HEADS, dtype=jnp.int32))  20.5 us
    dot_general x16, matrix products, head_partial(): jnp.einsum('rgd,kd->grk', grouped, key_cols, preferred_element_type=jnp.f...  17.1 us
    dynamic_slice x32, local copies, waits for them, and re-layouts, single_head(): lax.dynamic_slice_in_dim(piece_rows, key_value_head * (group_width * HEAD...  16.3 us
    all_to_all x1, blocking collectives, body(): lax.all_to_all(log_sum_exp[None], 'seq', split_axis=2, concat_axis=0, til...  9.87 us
  transfers between devices with their start and end apart: 3, of which 3 were waited for; matrix products, arithmetic and copies ran while one was open for 0% of the time, Pallas kernels for 0%

commit v1 on v0

v1 whole, which is shorter than its diff:
```python
import functools

import jax
import jax.numpy as jnp
from jax import lax
from jax.experimental import pallas as pl
from jax.experimental.pallas import tpu as pltpu
from jax.sharding import PartitionSpec as P

QUERY_HEADS = 32
KEY_VALUE_HEADS = 16
HEAD_SIZE = 128

score_scale = 168.0 ** (-0.5)
masked_value = -1e30
MESH = pl.DeviceIdType.MESH


def bit_of(index, bit):
    return (index // (1 << bit)) % 2


def flipped(index, mask):
    result = index
    bit = 0
    while (1 << bit) <= mask:
        if (mask >> bit) & 1:
            result = result + (1 - 2 * bit_of(index, bit)) * (1 << bit)
        bit += 1
    return result


def place_of(dest, order):
    place = 0
    for step, bit in enumerate(order):
        place = place + bit_of(dest, bit) * (1 << (len(order) - 1 - step))
    return place


def dest_at(place, order):
    dest = 0
    for step, bit in enumerate(order):
        dest = dest + bit_of(place, len(order) - 1 - step) * (1 << bit)
    return dest


def kernel(
    n, q_ref, live_ref, first_ref, k_hbm, v_hbm, w_hbm, out_ref,
    q_all, k_buf, v_buf, w_buf, part_a, part_b, lse_a, lse_b, got_a, got_b, gotl_a, gotl_b,
    acc, sent, came,
    load_sem, q_send, q_recv, p_send, p_recv, t_send, t_recv,
):
    me = lax.axis_index("seq")
    bits = n.bit_length() - 1
    orders = (list(range(bits)), [0] + list(range(2, bits)) + [1])
    per_dest = QUERY_HEADS // n
    group_width = QUERY_HEADS // KEY_VALUE_HEADS
    key_count = k_buf.shape[0]
    rows_each = q_ref.shape[1]
    rows = rows_each * n
    half_rows = rows // 2
    half_cols = q_ref.shape[2] // 2
    out_half = out_ref.shape[1] // 2
    parts, lses = (part_a, part_b), (lse_a, lse_b)
    gots, gotls = (got_a, got_b), (gotl_a, gotl_b)

    loads = [
        pltpu.make_async_copy(src, dst, load_sem.at[i])
        for i, (src, dst) in enumerate(((k_hbm, k_buf), (v_hbm, v_buf), (w_hbm, w_buf)))
    ]
    for load in loads:
        load.start()
    own = pltpu.make_async_copy(q_ref.at[0], q_all.at[me], load_sem.at[3])
    own.start()

    barrier = pltpu.get_barrier_semaphore()
    for bit in range(bits):
        pl.semaphore_signal(
            barrier, inc=1, device_id={"seq": flipped(me, 1 << bit)}, device_id_type=MESH
        )
    pl.semaphore_wait(barrier, bits)

    def q_copy(c, held, bit):
        cols = pl.ds(c * half_cols, half_cols)
        block = flipped(me, held)
        mask = held | (1 << bit)
        src = q_ref.at[0, :, cols] if held == 0 else q_all.at[block, :, cols]
        return pltpu.make_async_remote_copy(
            src_ref=src,
            dst_ref=q_all.at[block, :, cols],
            send_sem=q_send.at[c, mask],
            recv_sem=q_recv.at[c, mask],
            device_id={"seq": flipped(me, 1 << bit)},
            device_id_type=MESH,
        )

    def q_arrival(c, mask):
        cols = pl.ds(c * half_cols, half_cols)
        block = flipped(me, mask)
        return pltpu.make_async_remote_copy(
            src_ref=q_all.at[block, :, cols],
            dst_ref=q_all.at[block, :, cols],
            send_sem=q_send.at[c, mask],
            recv_sem=q_recv.at[c, mask],
            device_id={"seq": flipped(me, 1)},
            device_id_type=MESH,
        )

    walks = [[b for b in reversed(order) if b != 0] for order in orders]
    held = [[0], [0]]
    q_copies = []
    for step in range(bits - 1):
        for c in range(2):
            for mask in held[c]:
                copy = q_copy(c, mask, walks[c][step])
                copy.start()
                q_copies.append(copy)
        if step == 0:
            for c in range(2):
                copy = q_copy(c, 0, 0)
                copy.start()
                q_copies.append(copy)
        for c in range(2):
            new = [mask | (1 << walks[c][step]) for mask in held[c]]
            for mask in new:
                q_arrival(c, mask).wait_recv()
                copy = q_copy(c, mask, 0)
                copy.start()
                q_copies.append(copy)
            held[c] = held[c] + new
    for c in range(2):
        for mask in held[c]:
            q_arrival(c, mask | 1).wait_recv()
    own.wait()
    loads[0].wait()
    loads[1].wait()

    slot = lax.broadcasted_iota(jnp.int32, (key_count, rows), 0)
    row = lax.broadcasted_iota(jnp.int32, (key_count, rows), 1)
    allowed = (slot < live_ref[0]) & (me * key_count + slot <= first_ref[0] + row)

    def attend(i, start):
        place = start + i
        dest = dest_at(place // per_dest, orders[0])
        head = dest * per_dest + place % per_dest
        key_head = head // group_width
        q = q_all[:, :, pl.ds(pl.multiple_of(head * HEAD_SIZE, HEAD_SIZE), HEAD_SIZE)]
        q = q.reshape(rows, HEAD_SIZE)
        kv_cols = pl.ds(pl.multiple_of(key_head * HEAD_SIZE, HEAD_SIZE), HEAD_SIZE)
        scores = lax.dot_general(
            k_buf[:, kv_cols], q, (((1,), (1,)), ((), ())), preferred_element_type=jnp.float32
        ) * score_scale
        scores = jnp.where(allowed, scores, masked_value)
        best = jnp.max(scores, axis=0, keepdims=True)
        weights = jnp.where(allowed, jnp.exp(scores - best), 0.0)
        total = jnp.sum(weights, axis=0, keepdims=True)
        safe = jnp.where(total > 0, total, 1.0)
        weighted = lax.dot_general(
            v_buf[:, kv_cols], weights.astype(jnp.bfloat16), (((0,), (0,)), ((), ())),
            preferred_element_type=jnp.float32,
        )
        partial = (weighted * (1.0 / safe)).astype(jnp.bfloat16)
        lse = jnp.where(total > 0, best + jnp.log(safe), masked_value)
        for c in range(2):
            at = place_of(dest, orders[c]) * per_dest + place % per_dest
            parts[c][at] = partial[:, c * half_rows:(c + 1) * half_rows]
            lses[c][at] = lse[:, c * half_rows:(c + 1) * half_rows]
        return start

    def spans(c, step):
        base = 0
        for earlier in range(step):
            base = base + bit_of(me, orders[c][earlier]) * (n >> (earlier + 1))
        size = n >> (step + 1)
        mine = bit_of(me, orders[c][step])
        return base + (1 - mine) * size, base + mine * size, n - 2 * size, size

    def p_copies(c, step):
        away, _, landing, size = spans(c, step)
        src = pl.ds(away * per_dest, size * per_dest)
        dst = pl.ds(landing * per_dest, size * per_dest)
        return [
            pltpu.make_async_remote_copy(
                src_ref=source.at[src],
                dst_ref=target.at[dst],
                send_sem=p_send.at[c, step, i],
                recv_sem=p_recv.at[c, step, i],
                device_id={"seq": flipped(me, 1 << orders[c][step])},
                device_id_type=MESH,
            )
            for i, (source, target) in enumerate(((parts[c], gots[c]), (lses[c], gotls[c])))
        ]

    def merge(c, start, landing, count):
        def one(i, carry):
            at, came_at = start + i, landing + i
            left, right = lses[c][at], gotls[c][came_at]
            top = jnp.maximum(left, right)
            scale_l, scale_r = jnp.exp(left - top), jnp.exp(right - top)
            whole = scale_l + scale_r
            inverse = 1.0 / whole
            mixed = parts[c][at].astype(jnp.float32) * (scale_l * inverse) + gots[c][
                came_at
            ].astype(jnp.float32) * (scale_r * inverse)
            parts[c][at] = mixed.astype(jnp.bfloat16)
            lses[c][at] = top + jnp.log(whole)
            return carry

        lax.fori_loop(0, count, one, 0)

    half_heads = QUERY_HEADS // 2
    away0, keep0, _, _ = spans(0, 0)
    lax.fori_loop(0, half_heads, attend, away0 * per_dest)
    pending = []
    flying = [p_copies(c, 0) for c in range(2)]
    for copies in flying:
        for copy in copies:
            copy.start()
    lax.fori_loop(0, half_heads, attend, keep0 * per_dest)
    for step in range(bits):
        for c in range(2):
            _, keep, landing, size = spans(c, step)
            for copy in flying[c]:
                copy.wait_recv()
            pending += flying[c]
            merge(c, keep * per_dest, landing * per_dest, size * per_dest)
            if step + 1 < bits:
                flying[c] = p_copies(c, step + 1)
                for copy in flying[c]:
                    copy.start()

    loads[2].wait()
    merged = []
    for c in range(2):
        at = place_of(me, orders[c]) * per_dest
        merged.append(parts[c][pl.ds(at, per_dest)].reshape(per_dest * HEAD_SIZE, half_rows))

    def t_copy(c, step):
        away, _, landing, size = spans(c, step)
        return pltpu.make_async_remote_copy(
            src_ref=sent.at[c, pl.ds(away, size)],
            dst_ref=came.at[c, pl.ds(landing, size)],
            send_sem=t_send.at[c, step],
            recv_sem=t_recv.at[c, step],
            device_id={"seq": flipped(me, 1 << orders[c][step])},
            device_id_type=MESH,
        )

    def ship(c, step):
        away, _, _, size = spans(c, step)

        def one(i, carry):
            sent[c, away + i] = acc[c, away + i].astype(jnp.bfloat16)
            return carry

        lax.fori_loop(0, size, one, 0)
        copy = t_copy(c, step)
        copy.start()
        return copy

    flying = []
    for c in range(2):
        for r in range(2):
            term = lax.dot_general(
                merged[r], w_buf[:, c * out_half:(c + 1) * out_half], (((0,), (0,)), ((), ())),
                preferred_element_type=jnp.float32,
            )
            for j in range(n // 2):
                at = place_of(r * (n // 2) + j, orders[c])
                acc[c, at] = term[j * rows_each:(j + 1) * rows_each]
        flying.append(ship(c, 0))
    for step in range(bits):
        for c in range(2):
            _, keep, landing, size = spans(c, step)
            flying[c].wait_recv()
            pending.append(flying[c])

            def add(i, carry):
                acc[c, keep + i] = acc[c, keep + i] + came[c, landing + i].astype(jnp.float32)
                return carry

            lax.fori_loop(0, size, add, 0)
            if step + 1 < bits:
                flying[c] = ship(c, step + 1)
    for c in range(2):
        at = place_of(me, orders[c])
        out_ref[:, c * out_half:(c + 1) * out_half] = acc[c, at].astype(jnp.bfloat16)
    for copy in q_copies + pending:
        copy.wait_send()


def body(query_block, cache_keys, stored_values, live_counts, first_position, out_weight):
    n = lax.axis_size("seq")
    bits = n.bit_length() - 1
    rows_each, width = query_block.shape
    half_rows = rows_each * n // 2
    d_model = out_weight.shape[1]
    per_dest = QUERY_HEADS // n
    vmem = pl.BlockSpec(memory_space=pltpu.VMEM)
    smem = pl.BlockSpec(memory_space=pltpu.SMEM)
    anywhere = pl.BlockSpec(memory_space=pl.ANY)
    bf16, f32 = jnp.bfloat16, jnp.float32
    dma = pltpu.SemaphoreType.DMA
    return pl.pallas_call(
        functools.partial(kernel, n),
        out_shape=jax.ShapeDtypeStruct((rows_each, d_model), bf16),
        in_specs=[vmem, smem, smem, anywhere, anywhere, anywhere],
        out_specs=vmem,
        scratch_shapes=[
            pltpu.VMEM((n, rows_each, width), bf16),
            pltpu.VMEM(cache_keys.shape, bf16),
            pltpu.VMEM(stored_values.shape, bf16),
            pltpu.VMEM(out_weight.shape, bf16),
            pltpu.VMEM((QUERY_HEADS, HEAD_SIZE, half_rows), bf16),
            pltpu.VMEM((QUERY_HEADS, HEAD_SIZE, half_rows), bf16),
            pltpu.VMEM((QUERY_HEADS, 1, half_rows), f32),
            pltpu.VMEM((QUERY_HEADS, 1, half_rows), f32),
            pltpu.VMEM((QUERY_HEADS, HEAD_SIZE, half_rows), bf16),
            pltpu.VMEM((QUERY_HEADS, HEAD_SIZE, half_rows), bf16),
            pltpu.VMEM((QUERY_HEADS, 1, half_rows), f32),
            pltpu.VMEM((QUERY_HEADS, 1, half_rows), f32),
            pltpu.VMEM((2, n, rows_each, d_model // 2), f32),
            pltpu.VMEM((2, n, rows_each, d_model // 2), bf16),
            pltpu.VMEM((2, n, rows_each, d_model // 2), bf16),
            dma((4,)),
            dma((2, n)),
            dma((2, n)),
            dma((2, bits, 2)),
            dma((2, bits, 2)),
            dma((2, bits)),
            dma((2, bits)),
        ],
        compiler_params=pltpu.CompilerParams(
            collective_id=0, has_side_effects=True, vmem_limit_bytes=48 * 1024 * 1024
        ),
        name="attend_project",
    )(query_block[None], live_counts, first_position, cache_keys, stored_values, out_weight)


def solution(mesh):
    in_specs = (
        P(("groups", "seq"), None),
        P(("groups", "seq"), None),
        P(("groups", "seq"), None),
        P(("groups", "seq")),
        P("groups"),
        P("seq", None),
    )
    out_specs = P(("groups", "seq"), None)
    return jax.shard_map(body, mesh=mesh, in_specs=in_specs, out_specs=out_specs, check_vma=False)
```

time: 310 us -> 94 us (0.30)
  waiting for transfers between devices: 173 us -> 0 us
  Pallas kernels: 0 us -> 86.6 us
  matrix products: 49.7 us -> 0 us
  loops' own time: 20.5 us -> 0 us
  local copies, waits for them, and re-layouts: 25.9 us -> 5.79 us
  between operations: 14.9 us -> 1.32 us
  blocking collectives: 9.87 us -> 0 us
  other arithmetic: 9 us -> 0 us
  starting transfers between devices: 4.47 us -> 0 us
    pallas_call x0 -> x1, Pallas kernels: none -> 86.6 us  [body(): pl.pallas_call(functools.partial(kernel, n), out_shape=jax.ShapeDtypeStru...]
    reduce_scatter x1 -> x0, waiting for transfers between devices: 86.6 us -> none  [body(): lax.psum_scatter(jnp.dot(flattened, out_weight, preferred_element_type=jn...]
    dot_general x33 -> x0, matrix products: 49.7 us -> none  [the longest x16 29.2 us: head_partial(): jnp.einsum('grk,kd->grd', weights.astype(jnp.bfloat16), value_cols, prefe...]
    all_gather x1 -> x0, waiting for transfers between devices: 45 us -> none  [body(): piece_rows = lax.all_gather(query_block, 'seq', axis=0, tiled=True)]
    all_to_all x1 -> x0, waiting for transfers between devices: 40.8 us -> none  [body(): lax.all_to_all(value_partial_sum[None], 'seq', split_axis=2, concat_axis=...]
    dynamic_slice x48 -> x0, local copies, waits for them, and re-layouts: 25.8 us -> none  [the longest x32 16.3 us: single_head(): lax.dynamic_slice_in_dim(piece_rows, key_value_head * (group_width * HEAD...]
    another operation x1 -> x0, loops' own time: 20.5 us -> none  [body(): lax.map(single_head, jnp.arange(KEY_VALUE_HEADS, dtype=jnp.int32))]
    all_to_all x1 -> x0, blocking collectives: 9.87 us -> none  [body(): lax.all_to_all(log_sum_exp[None], 'seq', split_axis=2, concat_axis=0, til...]
  transfers between devices with their start and end apart: 3 -> 0, of which waited for: 3 -> 0; matrix products, arithmetic and copies ran while one was open for 0% -> 0% of each run, Pallas kernels for 0% -> 0%
where the time goes in v1:
time: 94 us; the launch traced here: 93.8 us
  Pallas kernels  86.6 us (92%)
  local copies, waits for them, and re-layouts  5.79 us (6%)
  between operations  1.32 us (1%)
    pallas_call x1, Pallas kernels, body(): pl.pallas_call(functools.partial(kernel, n), out_shape=jax.ShapeDtypeStru...  86.6 us
    unnamed x9, local copies, waits for them, and re-layouts  5.79 us

profile of v1, /device:TPU:0, one launch (start us, length us, event | category | flops | bytes accessed | tf_op | source)
XLA Modules:
  0.0 93.8 jit_solution(16079733668165550871)
XLA Ops:
  1.3 0.0 copy-start
  1.3 1.8 %copy-done = bf16[256,5376]{1,0:T(8,128)(2,1)S(1)} copy-done((bf16[256,5376]{1,0:T(8,128)(2,1)S(1)}, bf16[256,5376]{1,0:T(8,128)(2,1)}, u32[]{:S(2)}) %copy-start) | copy-done | bytes 2752536
  3.1 0.0 copy-start.1
  3.1 1.2 %copy-done.1 = bf16[256,2048]{1,0:T(8,128)(2,1)S(1)} copy-done((bf16[256,2048]{1,0:T(8,128)(2,1)S(1)}, bf16[256,2048]{1,0:T(8,128)(2,1)}, u32[]{:S(2)}) %copy-start.1) | copy-done | bytes 1048600
  4.3 0.0 copy-start.2
  4.3 1.2 %copy-done.2 = bf16[256,2048]{1,0:T(8,128)(2,1)S(1)} copy-done((bf16[256,2048]{1,0:T(8,128)(2,1)S(1)}, bf16[256,2048]{1,0:T(8,128)(2,1)}, u32[]{:S(2)}) %copy-start.2) | copy-done | bytes 1048600
  5.5 0.0 copy-start.3
  5.5 0.9 copy-done.3
  6.4 86.6 %attend_project.1 = bf16[16,5376]{1,0:T(8,128)(2,1)S(1)} custom-call(bf16[1,16,4096]{2,1,0:T(8,128)(2,1)S(1)} %bitcast.1, s32[1]{0:T(128)S(6)} %copy.8.live_ref, s32[1]{0:T(128)S(6)} %copy.9.first_ref, bf16[256,2048]{1,0:T(8,128)(2,1)S(1)} %copy-done.1, bf16[256,2048]{1,0:T(8,128)(2,1)S(1)} %copy-done.2, bf16[256,5376]{1,0:T(8,128)(2,1)S(1)} %copy-done), custom_call_target="tpu_custom_call" | custom-call | tf_op jit(solution)/shard_map/attend_project/pallas_call | solution.py:304
  93.1 0.7 copy.10
Async XLA Ops:
  1.3 1.8 %copy-start = (bf16[256,5376]{1,0:T(8,128)(2,1)S(1)}, bf16[256,5376]{1,0:T(8,128)(2,1)}, u32[]{:S(2)}) copy-start(bf16[256,5376]{1,0:T(8,128)(2,1)} %w_hbm.1) | copy-start | bytes 8257540
  3.1 1.2 %copy-start.1 = (bf16[256,2048]{1,0:T(8,128)(2,1)S(1)}, bf16[256,2048]{1,0:T(8,128)(2,1)}, u32[]{:S(2)}) copy-start(bf16[256,2048]{1,0:T(8,128)(2,1)} %k_hbm.1) | copy-start | bytes 3145732
  4.3 1.2 %copy-start.2 = (bf16[256,2048]{1,0:T(8,128)(2,1)S(1)}, bf16[256,2048]{1,0:T(8,128)(2,1)}, u32[]{:S(2)}) copy-start(bf16[256,2048]{1,0:T(8,128)(2,1)} %v_hbm.1) | copy-start | bytes 3145732
  5.5 0.9 copy-start.3

commit v2 on v1

--- a/solution.py
+++ b/solution.py
@@ -46,8 +46,7 @@
 
 def kernel(
     n, q_ref, live_ref, first_ref, k_hbm, v_hbm, w_hbm, out_ref,
-    q_all, k_buf, v_buf, w_buf, part_a, part_b, lse_a, lse_b, got_a, got_b, gotl_a, gotl_b,
-    acc, sent, came,
+    q_all, k_buf, v_buf, w_buf, parts, lses, gots, gotls, acc, sent, came,
     load_sem, q_send, q_recv, p_send, p_recv, t_send, t_recv,
 ):
     me = lax.axis_index("seq")
@@ -60,9 +59,8 @@
     rows = rows_each * n
     half_rows = rows // 2
     half_cols = q_ref.shape[2] // 2
-    out_half = out_ref.shape[1] // 2
-    parts, lses = (part_a, part_b), (lse_a, lse_b)
-    gots, gotls = (got_a, got_b), (gotl_a, gotl_b)
+    p_flows = parts.shape[0]
+    t_flows, out_part = acc.shape[0], acc.shape[3]
 
     loads = [
         pltpu.make_async_copy(src, dst, load_sem.at[i])
@@ -139,10 +137,9 @@
     row = lax.broadcasted_iota(jnp.int32, (key_count, rows), 1)
     allowed = (slot < live_ref[0]) & (me * key_count + slot <= first_ref[0] + row)
 
-    def attend(i, start):
-        place = start + i
-        dest = dest_at(place // per_dest, orders[0])
-        head = dest * per_dest + place % per_dest
+    def attend(sub, i, start):
+        dest = dest_at(start + i, orders[0])
+        head = dest * per_dest + sub
         key_head = head // group_width
         q = q_all[:, :, pl.ds(pl.multiple_of(head * HEAD_SIZE, HEAD_SIZE), HEAD_SIZE)]
         q = q.reshape(rows, HEAD_SIZE)
@@ -162,9 +159,9 @@
         partial = (weighted * (1.0 / safe)).astype(jnp.bfloat16)
         lse = jnp.where(total > 0, best + jnp.log(safe), masked_value)
         for c in range(2):
-            at = place_of(dest, orders[c]) * per_dest + place % per_dest
-            parts[c][at] = partial[:, c * half_rows:(c + 1) * half_rows]
-            lses[c][at] = lse[:, c * half_rows:(c + 1) * half_rows]
+            at = place_of(dest, orders[c])
+            parts[2 * sub + c, at] = partial[:, c * half_rows:(c + 1) * half_rows]
+            lses[2 * sub + c, at] = lse[:, c * half_rows:(c + 1) * half_rows]
         return start
 
     def spans(c, step):
@@ -175,116 +172,125 @@
         mine = bit_of(me, orders[c][step])
         return base + (1 - mine) * size, base + mine * size, n - 2 * size, size
 
-    def p_copies(c, step):
-        away, _, landing, size = spans(c, step)
-        src = pl.ds(away * per_dest, size * per_dest)
-        dst = pl.ds(landing * per_dest, size * per_dest)
+    def p_copies(f, step):
+        away, _, landing, size = spans(f % 2, step)
         return [
             pltpu.make_async_remote_copy(
-                src_ref=source.at[src],
-                dst_ref=target.at[dst],
-                send_sem=p_send.at[c, step, i],
-                recv_sem=p_recv.at[c, step, i],
-                device_id={"seq": flipped(me, 1 << orders[c][step])},
+                src_ref=source.at[f, pl.ds(away, size)],
+                dst_ref=target.at[f, pl.ds(landing, size)],
+                send_sem=p_send.at[f, step, i],
+                recv_sem=p_recv.at[f, step, i],
+                device_id={"seq": flipped(me, 1 << orders[f % 2][step])},
                 device_id_type=MESH,
             )
-            for i, (source, target) in enumerate(((parts[c], gots[c]), (lses[c], gotls[c])))
+            for i, (source, target) in enumerate(((parts, gots), (lses, gotls)))
         ]
 
-    def merge(c, start, landing, count):
+    def merge(f, start, landing, count):
         def one(i, carry):
             at, came_at = start + i, landing + i
-            left, right = lses[c][at], gotls[c][came_at]
+            left, right = lses[f, at], gotls[f, came_at]
             top = jnp.maximum(left, right)
             scale_l, scale_r = jnp.exp(left - top), jnp.exp(right - top)
             whole = scale_l + scale_r
             inverse = 1.0 / whole
-            mixed = parts[c][at].astype(jnp.float32) * (scale_l * inverse) + gots[c][
-                came_at
+            mixed = parts[f, at].astype(jnp.float32) * (scale_l * inverse) + gots[
+                f, came_at
             ].astype(jnp.float32) * (scale_r * inverse)
-            parts[c][at] = mixed.astype(jnp.bfloat16)
-            lses[c][at] = top + jnp.log(whole)
+            parts[f, at] = mixed.astype(jnp.bfloat16)
+            lses[f, at] = top + jnp.log(whole)
             return carry
 
-        lax.fori_loop(0, count, one, 0)
-
-    half_heads = QUERY_HEADS // 2
+        lax.fori_loop(0, count, one, 0, unroll=min(count, 4))
+
+    pending = []
+    flying = {}
+
+    def p_start(f, step):
+        flying[f] = p_copies(f, step)
+        for copy in flying[f]:
+            copy.start()
+
+    def p_turn(f, step):
+        _, keep, landing, size = spans(f % 2, step)
+        for copy in flying[f]:
+            copy.wait_recv()
+        pending.extend(flying[f])
+        merge(f, keep, landing, size)
+        if step + 1 < bits:
+            p_start(f, step + 1)
+
     away0, keep0, _, _ = spans(0, 0)
-    lax.fori_loop(0, half_heads, attend, away0 * per_dest)
-    pending = []
-    flying = [p_copies(c, 0) for c in range(2)]
-    for copies in flying:
-        for copy in copies:
-            copy.start()
-    lax.fori_loop(0, half_heads, attend, keep0 * per_dest)
-    for step in range(bits):
-        for c in range(2):
-            _, keep, landing, size = spans(c, step)
-            for copy in flying[c]:
-                copy.wait_recv()
-            pending += flying[c]
-            merge(c, keep * per_dest, landing * per_dest, size * per_dest)
-            if step + 1 < bits:
-                flying[c] = p_copies(c, step + 1)
-                for copy in flying[c]:
-                    copy.start()
+    for sub in range(per_dest):
+        lax.fori_loop(0, n // 2, functools.partial(attend, sub), away0, unroll=4)
+        p_start(2 * sub, 0)
+        p_start(2 * sub + 1, 0)
+    for sub in range(per_dest):
+        lax.fori_loop(0, n // 2, functools.partial(attend, sub), keep0, unroll=4)
+        p_turn(2 * sub, 0)
+        p_turn(2 * sub + 1, 0)
+    for step in range(1, bits):
+        for f in range(p_flows):
+            p_turn(f, step)
 
     loads[2].wait()
     merged = []
     for c in range(2):
-        at = place_of(me, orders[c]) * per_dest
-        merged.append(parts[c][pl.ds(at, per_dest)].reshape(per_dest * HEAD_SIZE, half_rows))
-
-    def t_copy(c, step):
-        away, _, landing, size = spans(c, step)
+        at = place_of(me, orders[c])
+        merged.append(
+            jnp.concatenate([parts[2 * sub + c, at] for sub in range(per_dest)], axis=0)
+        )
+
+    def t_copy(f, step):
+        away, _, landing, size = spans(f % 2, step)
         return pltpu.make_async_remote_copy(
-            src_ref=sent.at[c, pl.ds(away, size)],
-            dst_ref=came.at[c, pl.ds(landing, size)],
-            send_sem=t_send.at[c, step],
-            recv_sem=t_recv.at[c, step],
-            device_id={"seq": flipped(me, 1 << orders[c][step])},
+            src_ref=sent.at[f, pl.ds(away, size)],
+            dst_ref=came.at[f, pl.ds(landing, size)],
+            send_sem=t_send.at[f, step],
+            recv_sem=t_recv.at[f, step],
+            device_id={"seq": flipped(me, 1 << orders[f % 2][step])},
             device_id_type=MESH,
         )
 
-    def ship(c, step):
-        away, _, _, size = spans(c, step)
+    def ship(f, step):
+        away, _, _, size = spans(f % 2, step)
 
         def one(i, carry):
-            sent[c, away + i] = acc[c, away + i].astype(jnp.bfloat16)
+            sent[f, away + i] = acc[f, away + i].astype(jnp.bfloat16)
             return carry
 
-        lax.fori_loop(0, size, one, 0)
-        copy = t_copy(c, step)
+        lax.fori_loop(0, size, one, 0, unroll=min(size, 4))
+        copy = t_copy(f, step)
         copy.start()
         return copy
 
     flying = []
-    for c in range(2):
+    for f in range(t_flows):
         for r in range(2):
             term = lax.dot_general(
-                merged[r], w_buf[:, c * out_half:(c + 1) * out_half], (((0,), (0,)), ((), ())),
+                merged[r], w_buf[:, f * out_part:(f + 1) * out_part], (((0,), (0,)), ((), ())),
                 preferred_element_type=jnp.float32,
             )
             for j in range(n // 2):
-                at = place_of(r * (n // 2) + j, orders[c])
-                acc[c, at] = term[j * rows_each:(j + 1) * rows_each]
-        flying.append(ship(c, 0))
+                at = place_of(r * (n // 2) + j, orders[f % 2])
+                acc[f, at] = term[j * rows_each:(j + 1) * rows_each]
+        flying.append(ship(f, 0))
     for step in range(bits):
-        for c in range(2):
-            _, keep, landing, size = spans(c, step)
-            flying[c].wait_recv()
-            pending.append(flying[c])
+        for f in range(t_flows):
+            _, keep, landing, size = spans(f % 2, step)
+            flying[f].wait_recv()
+            pending.append(flying[f])
 
             def add(i, carry):
-                acc[c, keep + i] = acc[c, keep + i] + came[c, landing + i].astype(jnp.float32)
+                acc[f, keep + i] = acc[f, keep + i] + came[f, landing + i].astype(jnp.float32)
                 return carry
 
-            lax.fori_loop(0, size, add, 0)
+            lax.fori_loop(0, size, add, 0, unroll=min(size, 4))
             if step + 1 < bits:
-                flying[c] = ship(c, step + 1)
-    for c in range(2):
-        at = place_of(me, orders[c])
-        out_ref[:, c * out_half:(c + 1) * out_half] = acc[c, at].astype(jnp.bfloat16)
+                flying[f] = ship(f, step + 1)
+    for f in range(t_flows):
+        at = place_of(me, orders[f % 2])
+        out_ref[:, f * out_part:(f + 1) * out_part] = acc[f, at].astype(jnp.bfloat16)
     for copy in q_copies + pending:
         copy.wait_send()
 
@@ -296,6 +302,8 @@
     half_rows = rows_each * n // 2
     d_model = out_weight.shape[1]
     per_dest = QUERY_HEADS // n
+    p_flows = 2 * per_dest
+    t_flows = max(f for f in (2, 4, 6) if d_model % (128 * f) == 0)
     vmem = pl.BlockSpec(memory_space=pltpu.VMEM)
     smem = pl.BlockSpec(memory_space=pltpu.SMEM)
     anywhere = pl.BlockSpec(memory_space=pl.ANY)
@@ -304,34 +312,30 @@
     return pl.pallas_call(
         functools.partial(kernel, n),
         out_shape=jax.ShapeDtypeStruct((rows_each, d_model), bf16),
-        in_specs=[vmem, smem, smem, anywhere, anywhere, anywhere],
+        in_specs=[anywhere, smem, smem, anywhere, anywhere, anywhere],
         out_specs=vmem,
         scratch_shapes=[
             pltpu.VMEM((n, rows_each, width), bf16),
             pltpu.VMEM(cache_keys.shape, bf16),
             pltpu.VMEM(stored_values.shape, bf16),
             pltpu.VMEM(out_weight.shape, bf16),
-            pltpu.VMEM((QUERY_HEADS, HEAD_SIZE, half_rows), bf16),
-            pltpu.VMEM((QUERY_HEADS, HEAD_SIZE, half_rows), bf16),
-            pltpu.VMEM((QUERY_HEADS, 1, half_rows), f32),
-            pltpu.VMEM((QUERY_HEADS, 1, half_rows), f32),
-            pltpu.VMEM((QUERY_HEADS, HEAD_SIZE, half_rows), bf16),
-            pltpu.VMEM((QUERY_HEADS, HEAD_SIZE, half_rows), bf16),
-            pltpu.VMEM((QUERY_HEADS, 1, half_rows), f32),
-            pltpu.VMEM((QUERY_HEADS, 1, half_rows), f32),
-            pltpu.VMEM((2, n, rows_each, d_model // 2), f32),
-            pltpu.VMEM((2, n, rows_each, d_model // 2), bf16),
-            pltpu.VMEM((2, n, rows_each, d_model // 2), bf16),
+            pltpu.VMEM((p_flows, n, HEAD_SIZE, half_rows), bf16),
+            pltpu.VMEM((p_flows, n, 1, half_rows), f32),
+            pltpu.VMEM((p_flows, n, HEAD_SIZE, half_rows), bf16),
+            pltpu.VMEM((p_flows, n, 1, half_rows), f32),
+            pltpu.VMEM((t_flows, n, rows_each, d_model // t_flows), f32),
+            pltpu.VMEM((t_flows, n, rows_each, d_model // t_flows), bf16),
+            pltpu.VMEM((t_flows, n, rows_each, d_model // t_flows), bf16),
             dma((4,)),
             dma((2, n)),
             dma((2, n)),
-            dma((2, bits, 2)),
-            dma((2, bits, 2)),
-            dma((2, bits)),
-            dma((2, bits)),
+            dma((p_flows, bits, 2)),
+            dma((p_flows, bits, 2)),
+            dma((t_flows, bits)),
+            dma((t_flows, bits)),
         ],
         compiler_params=pltpu.CompilerParams(
-            collective_id=0, has_side_effects=True, vmem_limit_bytes=48 * 1024 * 1024
+            collective_id=0, has_side_effects=True, vmem_limit_bytes=63 * 1024 * 1024
         ),
         name="attend_project",
     )(query_block[None], live_counts, first_position, cache_keys, stored_values, out_weight)

time: 94 us -> 78.9 us (0.84)
  Pallas kernels: 86.6 us -> 75.8 us
  local copies, waits for them, and re-layouts: 5.79 us -> 1.6 us
    pallas_call x1, Pallas kernels: 86.6 us -> 75.8 us  [body(): pl.pallas_call(functools.partial(kernel, n), out_shape=jax.ShapeDtypeStru...]
    unnamed x9 -> x1, local copies, waits for them, and re-layouts: 5.79 us -> 1.6 us
where the time goes in v2:
time: 78.9 us; the launch traced here: 78.7 us
  Pallas kernels  75.8 us (96%)
  local copies, waits for them, and re-layouts  1.6 us (2%)
  between operations  1.3 us (2%)
    pallas_call x1, Pallas kernels, body(): pl.pallas_call(functools.partial(kernel, n), out_shape=jax.ShapeDtypeStru...  75.8 us
    unnamed x1, local copies, waits for them, and re-layouts  1.6 us

profile of v2, /device:TPU:0, one launch (start us, length us, event | category | flops | bytes accessed | tf_op | source)
XLA Modules:
  0.0 78.7 jit_solution(17198450747807178058)
XLA Ops:
  1.3 75.8 %attend_project.1 = bf16[16,5376]{1,0:T(8,128)(2,1)} custom-call(bf16[1,16,4096]{2,1,0:T(8,128)(2,1)} %bitcast.1, s32[1]{0:T(128)S(6)} %copy.8.live_ref, s32[1]{0:T(128)S(6)} %copy.9.first_ref, bf16[256,2048]{1,0:T(8,128)(2,1)} %k_hbm.1, bf16[256,2048]{1,0:T(8,128)(2,1)} %v_hbm.1, bf16[256,5376]{1,0:T(8,128)(2,1)} %w_hbm.1), custom_call_target="tpu_custom_call" | custom-call | tf_op jit(solution)/shard_map/attend_project/pallas_call | solution.py:312
  77.1 1.6 %copy.10 = bf16[16,5376]{1,0:T(8,128)(2,1)} copy(bf16[16,5376]{1,0:T(8,128)(2,1)} %attend_project.1) | data formatting | bytes 344064

commit v3 on v2

--- a/solution.py
+++ b/solution.py
@@ -47,7 +47,7 @@
 def kernel(
     n, q_ref, live_ref, first_ref, k_hbm, v_hbm, w_hbm, out_ref,
     q_all, k_buf, v_buf, w_buf, parts, lses, gots, gotls, acc, sent, came,
-    load_sem, q_send, q_recv, p_send, p_recv, t_send, t_recv,
+    load_sem, own_sem, q_send, q_recv, p_send, p_recv, t_send, t_recv,
 ):
     me = lax.axis_index("seq")
     bits = n.bit_length() - 1
@@ -58,7 +58,7 @@
     rows_each = q_ref.shape[1]
     rows = rows_each * n
     half_rows = rows // 2
-    half_cols = q_ref.shape[2] // 2
+    half_dests = n // 2
     p_flows = parts.shape[0]
     t_flows, out_part = acc.shape[0], acc.shape[3]
 
@@ -66,10 +66,19 @@
         pltpu.make_async_copy(src, dst, load_sem.at[i])
         for i, (src, dst) in enumerate(((k_hbm, k_buf), (v_hbm, v_buf), (w_hbm, w_buf)))
     ]
-    for load in loads:
-        load.start()
-    own = pltpu.make_async_copy(q_ref.at[0], q_all.at[me], load_sem.at[3])
-    own.start()
+    own = []
+    for sub in range(per_dest):
+        for dest in range(n):
+            head = dest * per_dest + sub
+            own.append(
+                pltpu.make_async_copy(
+                    q_ref.at[0, :, pl.ds(head * HEAD_SIZE, HEAD_SIZE)],
+                    q_all.at[me, sub * n + dest],
+                    own_sem.at[head],
+                )
+            )
+    for copy in own + loads:
+        copy.start()
 
     barrier = pltpu.get_barrier_semaphore()
     for bit in range(bits):
@@ -78,58 +87,73 @@
         )
     pl.semaphore_wait(barrier, bits)
 
-    def q_copy(c, held, bit):
-        cols = pl.ds(c * half_cols, half_cols)
+    walks = [[b for b in reversed(order) if b != 0] for order in orders]
+    q_copies = []
+
+    def q_copy(sub, c, held, bit):
+        heads = pl.ds(sub * n + c * half_dests, half_dests)
         block = flipped(me, held)
         mask = held | (1 << bit)
-        src = q_ref.at[0, :, cols] if held == 0 else q_all.at[block, :, cols]
         return pltpu.make_async_remote_copy(
-            src_ref=src,
-            dst_ref=q_all.at[block, :, cols],
-            send_sem=q_send.at[c, mask],
-            recv_sem=q_recv.at[c, mask],
+            src_ref=q_all.at[block, heads],
+            dst_ref=q_all.at[block, heads],
+            send_sem=q_send.at[2 * sub + c, mask],
+            recv_sem=q_recv.at[2 * sub + c, mask],
             device_id={"seq": flipped(me, 1 << bit)},
             device_id_type=MESH,
         )
 
-    def q_arrival(c, mask):
-        cols = pl.ds(c * half_cols, half_cols)
+    def q_forward(sub, c, held, step):
+        for bit in walks[c][step:] + [0]:
+            copy = q_copy(sub, c, held, bit)
+            copy.start()
+            q_copies.append(copy)
+
+    def q_arrival(sub, c, mask):
+        heads = pl.ds(sub * n + c * half_dests, half_dests)
         block = flipped(me, mask)
-        return pltpu.make_async_remote_copy(
-            src_ref=q_all.at[block, :, cols],
-            dst_ref=q_all.at[block, :, cols],
-            send_sem=q_send.at[c, mask],
-            recv_sem=q_recv.at[c, mask],
+        pltpu.make_async_remote_copy(
+            src_ref=q_all.at[block, heads],
+            dst_ref=q_all.at[block, heads],
+            send_sem=q_send.at[2 * sub + c, mask],
+            recv_sem=q_recv.at[2 * sub + c, mask],
             device_id={"seq": flipped(me, 1)},
             device_id_type=MESH,
-        )
-
-    walks = [[b for b in reversed(order) if b != 0] for order in orders]
-    held = [[0], [0]]
-    q_copies = []
-    for step in range(bits - 1):
+        ).wait_recv()
+
+    def held_before(c, step):
+        masks = [0]
+        for bit in walks[c][:step]:
+            masks = masks + [mask | (1 << bit) for mask in masks]
+        return masks
+
+    def q_turn(sub, step):
         for c in range(2):
-            for mask in held[c]:
-                copy = q_copy(c, mask, walks[c][step])
-                copy.start()
-                q_copies.append(copy)
-        if step == 0:
-            for c in range(2):
-                copy = q_copy(c, 0, 0)
-                copy.start()
-                q_copies.append(copy)
+            for held in held_before(c, step):
+                mask = held | (1 << walks[c][step])
+                q_arrival(sub, c, mask)
+                q_forward(sub, c, mask, step + 1)
+
+    def q_finish(sub):
         for c in range(2):
-            new = [mask | (1 << walks[c][step]) for mask in held[c]]
-            for mask in new:
-                q_arrival(c, mask).wait_recv()
-                copy = q_copy(c, mask, 0)
-                copy.start()
-                q_copies.append(copy)
-            held[c] = held[c] + new
+            for held in held_before(c, bits - 1):
+                q_arrival(sub, c, held | 1)
+
+    for copy in own:
+        copy.wait()
     for c in range(2):
-        for mask in held[c]:
-            q_arrival(c, mask | 1).wait_recv()
-    own.wait()
+        q_forward(0, c, 0, 0)
+    for step in range(bits - 2):
+        q_turn(0, step)
+        for sub in range(1, per_dest):
+            if step == 0:
+                for c in range(2):
+                    q_forward(sub, c, 0, 0)
+            else:
+                q_turn(sub, step - 1)
+    q_turn(0, bits - 2)
+    for sub in range(1, per_dest):
+        q_turn(sub, bits - 3)
     loads[0].wait()
     loads[1].wait()
 
@@ -141,8 +165,7 @@
         dest = dest_at(start + i, orders[0])
         head = dest * per_dest + sub
         key_head = head // group_width
-        q = q_all[:, :, pl.ds(pl.multiple_of(head * HEAD_SIZE, HEAD_SIZE), HEAD_SIZE)]
-        q = q.reshape(rows, HEAD_SIZE)
+        q = q_all[:, sub * n + dest].reshape(rows, HEAD_SIZE)
         kv_cols = pl.ds(pl.multiple_of(key_head * HEAD_SIZE, HEAD_SIZE), HEAD_SIZE)
         scores = lax.dot_general(
             k_buf[:, kv_cols], q, (((1,), (1,)), ((), ())), preferred_element_type=jnp.float32
@@ -221,17 +244,28 @@
             p_start(f, step + 1)
 
     away0, keep0, _, _ = spans(0, 0)
+    turned = [0] * p_flows
+
+    def p_advance(sub, step):
+        for f in (2 * sub, 2 * sub + 1):
+            if turned[f] == step:
+                p_turn(f, step)
+                turned[f] += 1
+
     for sub in range(per_dest):
+        q_finish(sub)
         lax.fori_loop(0, n // 2, functools.partial(attend, sub), away0, unroll=4)
         p_start(2 * sub, 0)
         p_start(2 * sub + 1, 0)
-    for sub in range(per_dest):
+        if sub + 1 < per_dest:
+            q_turn(sub + 1, bits - 2)
+        if sub > 0:
+            p_advance(sub - 1, 0)
         lax.fori_loop(0, n // 2, functools.partial(attend, sub), keep0, unroll=4)
-        p_turn(2 * sub, 0)
-        p_turn(2 * sub + 1, 0)
-    for step in range(1, bits):
-        for f in range(p_flows):
-            p_turn(f, step)
+    for wave in range(bits + per_dest - 1):
+        for sub in range(per_dest):
+            if 0 <= wave - sub < bits:
+                p_advance(sub, wave - sub)
 
     loads[2].wait()
     merged = []
@@ -298,7 +332,7 @@
 def body(query_block, cache_keys, stored_values, live_counts, first_position, out_weight):
     n = lax.axis_size("seq")
     bits = n.bit_length() - 1
-    rows_each, width = query_block.shape
+    rows_each = query_block.shape[0]
     half_rows = rows_each * n // 2
     d_model = out_weight.shape[1]
     per_dest = QUERY_HEADS // n
@@ -315,7 +349,7 @@
         in_specs=[anywhere, smem, smem, anywhere, anywhere, anywhere],
         out_specs=vmem,
         scratch_shapes=[
-            pltpu.VMEM((n, rows_each, width), bf16),
+            pltpu.VMEM((n, QUERY_HEADS, rows_each, HEAD_SIZE), bf16),
             pltpu.VMEM(cache_keys.shape, bf16),
             pltpu.VMEM(stored_values.shape, bf16),
             pltpu.VMEM(out_weight.shape, bf16),
@@ -326,9 +360,10 @@
             pltpu.VMEM((t_flows, n, rows_each, d_model // t_flows), f32),
             pltpu.VMEM((t_flows, n, rows_each, d_model // t_flows), bf16),
             pltpu.VMEM((t_flows, n, rows_each, d_model // t_flows), bf16),
-            dma((4,)),
-            dma((2, n)),
-            dma((2, n)),
+            dma((3,)),
+            dma((QUERY_HEADS,)),
+            dma((p_flows, n)),
+            dma((p_flows, n)),
             dma((p_flows, bits, 2)),
             dma((p_flows, bits, 2)),
             dma((t_flows, bits)),

time: 78.9 us -> 76.5 us (0.970)
  Pallas kernels: 75.8 us -> 73.5 us
    pallas_call x1, Pallas kernels: 75.8 us -> 73.5 us  [body(): pl.pallas_call(functools.partial(kernel, n), out_shape=jax.ShapeDtypeStru...]
where the time goes in v3:
time: 76.5 us; the launch traced here: 76.4 us
  Pallas kernels  73.5 us (96%)
  local copies, waits for them, and re-layouts  1.6 us (2%)
  between operations  1.3 us (2%)
    pallas_call x1, Pallas kernels, body(): pl.pallas_call(functools.partial(kernel, n), out_shape=jax.ShapeDtypeStru...  73.5 us
    unnamed x1, local copies, waits for them, and re-layouts  1.6 us

profile of v3, /device:TPU:0, one launch (start us, length us, event | category | flops | bytes accessed | tf_op | source)
XLA Modules:
  0.0 76.4 jit_solution(2452312373623103255)
XLA Ops:
  1.3 73.5 %attend_project.1 = bf16[16,5376]{1,0:T(8,128)(2,1)} custom-call(bf16[1,16,4096]{2,1,0:T(8,128)(2,1)} %bitcast.1, s32[1]{0:T(128)S(6)} %copy.8.live_ref, s32[1]{0:T(128)S(6)} %copy.9.first_ref, bf16[256,2048]{1,0:T(8,128)(2,1)} %k_hbm.1, bf16[256,2048]{1,0:T(8,128)(2,1)} %v_hbm.1, bf16[256,5376]{1,0:T(8,128)(2,1)} %w_hbm.1), custom_call_target="tpu_custom_call" | custom-call | tf_op jit(solution)/shard_map/attend_project/pallas_call | solution.py:346
  74.8 1.6 %copy.10 = bf16[16,5376]{1,0:T(8,128)(2,1)} copy(bf16[16,5376]{1,0:T(8,128)(2,1)} %attend_project.1) | data formatting | bytes 344064

commit v4 on v3

--- a/solution.py
+++ b/solution.py
@@ -42,6 +42,10 @@
     for step, bit in enumerate(order):
         dest = dest + bit_of(place, len(order) - 1 - step) * (1 << bit)
     return dest
+
+
+def side_of(flow):
+    return 1 if flow == 1 else 0
 
 
 def kernel(
@@ -104,7 +108,7 @@
         )
 
     def q_forward(sub, c, held, step):
-        for bit in walks[c][step:] + [0]:
+        for bit in walks[side_of(2 * sub + c)][step:] + [0]:
             copy = q_copy(sub, c, held, bit)
             copy.start()
             q_copies.append(copy)
@@ -121,22 +125,23 @@
             device_id_type=MESH,
         ).wait_recv()
 
-    def held_before(c, step):
+    def held_before(side, step):
         masks = [0]
-        for bit in walks[c][:step]:
+        for bit in walks[side][:step]:
             masks = masks + [mask | (1 << bit) for mask in masks]
         return masks
 
     def q_turn(sub, step):
         for c in range(2):
-            for held in held_before(c, step):
-                mask = held | (1 << walks[c][step])
+            side = side_of(2 * sub + c)
+            for held in held_before(side, step):
+                mask = held | (1 << walks[side][step])
                 q_arrival(sub, c, mask)
                 q_forward(sub, c, mask, step + 1)
 
     def q_finish(sub):
         for c in range(2):
-            for held in held_before(c, bits - 1):
+            for held in held_before(0, bits - 1):
                 q_arrival(sub, c, held | 1)
 
     for copy in own:
@@ -182,7 +187,7 @@
         partial = (weighted * (1.0 / safe)).astype(jnp.bfloat16)
         lse = jnp.where(total > 0, best + jnp.log(safe), masked_value)
         for c in range(2):
-            at = place_of(dest, orders[c])
+            at = place_of(dest, orders[side_of(2 * sub + c)])
             parts[2 * sub + c, at] = partial[:, c * half_rows:(c + 1) * half_rows]
             lses[2 * sub + c, at] = lse[:, c * half_rows:(c + 1) * half_rows]
         return start
@@ -196,14 +201,14 @@
         return base + (1 - mine) * size, base + mine * size, n - 2 * size, size
 
     def p_copies(f, step):
-        away, _, landing, size = spans(f % 2, step)
+        away, _, landing, size = spans(side_of(f), step)
         return [
             pltpu.make_async_remote_copy(
                 src_ref=source.at[f, pl.ds(away, size)],
                 dst_ref=target.at[f, pl.ds(landing, size)],
                 send_sem=p_send.at[f, step, i],
                 recv_sem=p_recv.at[f, step, i],
-                device_id={"seq": flipped(me, 1 << orders[f % 2][step])},
+                device_id={"seq": flipped(me, 1 << orders[side_of(f)][step])},
                 device_id_type=MESH,
             )
             for i, (source, target) in enumerate(((parts, gots), (lses, gotls)))
@@ -235,7 +240,7 @@
             copy.start()
 
     def p_turn(f, step):
-        _, keep, landing, size = spans(f % 2, step)
+        _, keep, landing, size = spans(side_of(f), step)
         for copy in flying[f]:
             copy.wait_recv()
         pending.extend(flying[f])
@@ -270,24 +275,29 @@
     loads[2].wait()
     merged = []
     for c in range(2):
-        at = place_of(me, orders[c])
         merged.append(
-            jnp.concatenate([parts[2 * sub + c, at] for sub in range(per_dest)], axis=0)
+            jnp.concatenate(
+                [
+                    parts[f, place_of(me, orders[side_of(f)])]
+                    for f in range(c, p_flows, 2)
+                ],
+                axis=0,
+            )
         )
 
     def t_copy(f, step):
-        away, _, landing, size = spans(f % 2, step)
+        away, _, landing, size = spans(side_of(f), step)
         return pltpu.make_async_remote_copy(
             src_ref=sent.at[f, pl.ds(away, size)],
             dst_ref=came.at[f, pl.ds(landing, size)],
             send_sem=t_send.at[f, step],
             recv_sem=t_recv.at[f, step],
-            device_id={"seq": flipped(me, 1 << orders[f % 2][step])},
+            device_id={"seq": flipped(me, 1 << orders[side_of(f)][step])},
             device_id_type=MESH,
         )
 
     def ship(f, step):
-        away, _, _, size = spans(f % 2, step)
+        away, _, _, size = spans(side_of(f), step)
 
         def one(i, carry):
             sent[f, away + i] = acc[f, away + i].astype(jnp.bfloat16)
@@ -306,12 +316,12 @@
                 preferred_element_type=jnp.float32,
             )
             for j in range(n // 2):
-                at = place_of(r * (n // 2) + j, orders[f % 2])
+                at = place_of(r * (n // 2) + j, orders[side_of(f)])
                 acc[f, at] = term[j * rows_each:(j + 1) * rows_each]
         flying.append(ship(f, 0))
     for step in range(bits):
         for f in range(t_flows):
-            _, keep, landing, size = spans(f % 2, step)
+            _, keep, landing, size = spans(side_of(f), step)
             flying[f].wait_recv()
             pending.append(flying[f])
 
@@ -323,7 +333,7 @@
             if step + 1 < bits:
                 flying[f] = ship(f, step + 1)
     for f in range(t_flows):
-        at = place_of(me, orders[f % 2])
+        at = place_of(me, orders[side_of(f)])
         out_ref[:, f * out_part:(f + 1) * out_part] = acc[f, at].astype(jnp.bfloat16)
     for copy in q_copies + pending:
         copy.wait_send()

time: 76.5 us -> 76.1 us (level)
  no operation moved by 1% of the time
where the time goes in v4:
time: 76.1 us; the launch traced here: 76 us
  Pallas kernels  73.1 us (96%)
  local copies, waits for them, and re-layouts  1.6 us (2%)
  between operations  1.3 us (2%)
    pallas_call x1, Pallas kernels, body(): pl.pallas_call(functools.partial(kernel, n), out_shape=jax.ShapeDtypeStru...  73.1 us
    unnamed x1, local copies, waits for them, and re-layouts  1.6 us

profile of v4, /device:TPU:0, one launch (start us, length us, event | category | flops | bytes accessed | tf_op | source)
XLA Modules:
  0.0 76.0 jit_solution(7067816666889766385)
XLA Ops:
  1.3 73.1 %attend_project.1 = bf16[16,5376]{1,0:T(8,128)(2,1)} custom-call(bf16[1,16,4096]{2,1,0:T(8,128)(2,1)} %bitcast.1, s32[1]{0:T(128)S(6)} %copy.8.live_ref, s32[1]{0:T(128)S(6)} %copy.9.first_ref, bf16[256,2048]{1,0:T(8,128)(2,1)} %k_hbm.1, bf16[256,2048]{1,0:T(8,128)(2,1)} %v_hbm.1, bf16[256,5376]{1,0:T(8,128)(2,1)} %w_hbm.1), custom_call_target="tpu_custom_call" | custom-call | tf_op jit(solution)/shard_map/attend_project/pallas_call | solution.py:356
  74.4 1.6 %copy.10 = bf16[16,5376]{1,0:T(8,128)(2,1)} copy(bf16[16,5376]{1,0:T(8,128)(2,1)} %attend_project.1) | data formatting | bytes 344064

commit v5 on v4

--- a/solution.py
+++ b/solution.py
@@ -45,7 +45,7 @@
 
 
 def side_of(flow):
-    return 1 if flow == 1 else 0
+    return 1 if flow in (1, 4) else 0
 
 
 def kernel(

time: 76.1 us -> 73.6 us (0.967)
  Pallas kernels: 73.1 us -> 70.6 us
    pallas_call x1, Pallas kernels: 73.1 us -> 70.6 us  [body(): pl.pallas_call(functools.partial(kernel, n), out_shape=jax.ShapeDtypeStru...]
where the time goes in v5:
time: 73.6 us; the launch traced here: 73.5 us
  Pallas kernels  70.6 us (96%)
  local copies, waits for them, and re-layouts  1.6 us (2%)
  between operations  1.3 us (2%)
    pallas_call x1, Pallas kernels, body(): pl.pallas_call(functools.partial(kernel, n), out_shape=jax.ShapeDtypeStru...  70.6 us
    unnamed x1, local copies, waits for them, and re-layouts  1.6 us

profile of v5, /device:TPU:0, one launch (start us, length us, event | category | flops | bytes accessed | tf_op | source)
XLA Modules:
  0.0 73.5 jit_solution(2136837384631840782)
XLA Ops:
  1.3 70.6 %attend_project.1 = bf16[16,5376]{1,0:T(8,128)(2,1)} custom-call(bf16[1,16,4096]{2,1,0:T(8,128)(2,1)} %bitcast.1, s32[1]{0:T(128)S(6)} %copy.8.live_ref, s32[1]{0:T(128)S(6)} %copy.9.first_ref, bf16[256,2048]{1,0:T(8,128)(2,1)} %k_hbm.1, bf16[256,2048]{1,0:T(8,128)(2,1)} %v_hbm.1, bf16[256,5376]{1,0:T(8,128)(2,1)} %w_hbm.1), custom_call_target="tpu_custom_call" | custom-call | tf_op jit(solution)/shard_map/attend_project/pallas_call | solution.py:356
  71.9 1.6 %copy.10 = bf16[16,5376]{1,0:T(8,128)(2,1)} copy(bf16[16,5376]{1,0:T(8,128)(2,1)} %attend_project.1) | data formatting | bytes 344064
